TPU v7x, 32 devices: a whole 2x2x4 slice. The times are simulated.
32 devices in a mesh: wide: 8 (over z, y), narrow: 4 (over x, core).
Axes of the slice: x: 2, y: 2, z: 4, core: 2. Of those that a mesh axis runs over, the one named last changes fastest.
Arguments:
- entry_factor: bfloat16 [288, 4, 64, 1024], P('wide', 'narrow'), may hold values from -6 to 6
- entry_panel: int32 [288, 4], P('wide', 'narrow'), may hold values from 0 to 1
- entry_target: int32 [288, 4], P('wide', 'narrow'), may hold values from 0 to 7, as said below
- entry_count: int32 [4, 8], P('narrow', 'wide'), may hold values from 1 to 36, 96 in all within a row
- panel_shared: bfloat16 [16, 64, 1024], P('wide', None, 'narrow'), may hold values from -0.1875 to 0.1875
- coupling: float32 [16, 64, 64], P('wide'), may hold values from -0.75 to 0.75
- probes: bfloat16 [32, 64, 1024], P('narrow'), may hold values from -6 to 6
Outputs:
- left_factor: float32 [32, 64, 1024], P('narrow', None, 'wide')
- right_factor: float32 [32, 64, 1024], P('narrow', None, 'wide')
Inputs may be any that keep to these rules, and one draw needn't show every extreme that they name: `entry_panel`: the local panel of an entry of any slot, live or not. `entry_target`: the local target of an entry; every target has at least one live entry. `entry_count`: the live slots of one device; for every owner the counts over the 8 wide indices sum to 96, and some device holds exactly 36.
All inputs are finite; a program needn't handle non-finite values.
Results may differ from a plain program's by a relative error of at most 0.0036.
Values may be sent and summed in bfloat16 or wider, within the bound.
A program may use at most 64 MiB of HBM per device.

v0:
```python
import math
import jax
import jax.numpy as jnp
from jax import lax
from jax.sharding import PartitionSpec as P


def shards(entry_factor, entry_panel, entry_target, entry_count, panel_shared, coupling, probes):
    highest = lax.Precision.HIGHEST
    factors = entry_factor[:, 0]
    slot_count = factors.shape[0]
    rank_dim = factors.shape[1]
    full_width = factors.shape[2]
    panel_count = panel_shared.shape[0]
    target_count = probes.shape[0]
    live_mask = (jnp.arange(slot_count) < entry_count[0, 0]).astype(jnp.float32)
    pick_panel = (entry_panel == jnp.arange(panel_count)[None, :]).astype(jnp.float32) * live_mask[
        :, None
    ]
    pick_target = (entry_target == jnp.arange(target_count)[None, :]).astype(jnp.float32)
    pair_pick = (pick_panel[:, :, None] * pick_target[:, None, :]).reshape(
        slot_count, panel_count * target_count
    )
    gathered = lax.all_gather(panel_shared, "narrow", axis=2, tiled=True)
    projected = jnp.einsum("drb,tkb->dtrk", gathered, probes, preferred_element_type=jnp.float32)
    coefficients = jnp.einsum("dij,dtjk->dtik", coupling, projected, precision=highest).astype(
        jnp.bfloat16
    )
    coeff_table = coefficients.reshape(panel_count * target_count, rank_dim * rank_dim)
    chosen = jnp.dot(
        pair_pick.astype(jnp.bfloat16), coeff_table, preferred_element_type=jnp.float32
    )
    chosen = chosen.astype(jnp.bfloat16).reshape(slot_count, rank_dim, rank_dim)
    contributions = jnp.einsum("eji,ejb->eib", chosen, factors, preferred_element_type=jnp.float32)
    sketch = jnp.einsum("et,eib->tib", pick_target, contributions, precision=highest)
    wide_count = lax.axis_size("wide")
    share_cols = full_width // wide_count
    sketch_sum = lax.psum(sketch, "wide")
    gram_matrix = jnp.einsum("tib,tjb->tij", sketch_sum, sketch_sum, precision=highest)
    lower_factor = jnp.linalg.cholesky(gram_matrix)
    basis = jax.scipy.linalg.solve_triangular(lower_factor, sketch_sum, lower=True)
    basis_round = basis.astype(jnp.bfloat16)
    own_basis = lax.dynamic_slice_in_dim(basis, lax.axis_index("wide") * share_cols, share_cols, 2)
    selected = jnp.einsum(
        "et,tkb->ekb",
        pick_target.astype(jnp.bfloat16),
        basis_round,
        preferred_element_type=jnp.float32,
    )
    selected = selected.astype(jnp.bfloat16)
    back_terms = jnp.einsum("eib,ekb->eik", factors, selected, preferred_element_type=jnp.float32)
    summed = jnp.einsum("ep,eik->pik", pair_pick, back_terms, precision=highest)
    summed = summed.reshape(panel_count, target_count, rank_dim, rank_dim)
    middle_terms = jnp.einsum("dtik,dij->dtkj", summed, coupling, precision=highest)
    partial_rows = jnp.einsum(
        "dtkj,djb->tkb", middle_terms, gathered.astype(jnp.float32), precision=highest
    )
    coeff_part = lax.psum_scatter(partial_rows, "wide", scatter_dimension=2, tiled=True)
    root_width = math.sqrt(full_width)
    return (own_basis * root_width, coeff_part / root_width)


def solution(mesh):
    placed = (
        P("wide", "narrow", None, None),
        P("wide", "narrow"),
        P("wide", "narrow"),
        P("narrow", "wide"),
        P("wide", None, "narrow"),
        P("wide", None, None),
        P("narrow", None, None),
    )
    return jax.shard_map(
        shards,
        mesh=mesh,
        in_specs=placed,
        out_specs=(P("narrow", None, "wide"), P("narrow", None, "wide")),
        check_vma=False,
    )
```

profile of v0, /device:TPU:0, one launch (start us, length us, event | category | flops | bytes accessed | tf_op | source)
XLA Modules:
  0.0 328.4 jit_solution(10725598671400621314)
XLA Ops:
  7.2 0.7 fusion.36
  8.0 7.4 %all_gather.3 = bf16[2,64,1024]{2,1,0:T(8,128)(2,1)S(1)} all-gather(bf16[2,64,256]{2,1,0:T(8,128)(2,1)} %param.11), channel_id=1, replica_groups=mesh['wide'=8,'narrow'=4] {'narrow'}, dimensions={2}, use_global_device_ids=true | all-gather | bytes 327680 | tf_op jit(solution)/shard_map/all_gather | solution.py:24
  15.4 0.5 convolution_bitcast_fusion.1
  16.1 0.6 fusion.18
  18.1 0.6 reshape.99
  18.8 3.8 %fusion.4 = f32[36,64,1024]{2,1,0:T(8,128)S(1)} fusion(bf16[36,64,64]{2,1,0:T(8,128)(2,1)S(1)} %reshape.99, bf16[36,1,64,1024]{3,2,1,0:T(8,128)(2,1)} %param.7), kind=kOutput, calls=%fused_computation.4 | convolution fusion | flops 301989888 | bytes 14450688 | tf_op jit(solution)/shard_map/eji,ejb->eib/dot_general | solution.py:34
  22.6 10.1 %fusion = f32[8,64,1024]{2,0,1:T(8,128)} fusion(f32[36,64,1024]{2,1,0:T(8,128)S(1)} %fusion.4, s32[36]{0:T(128)S(1)} %bitcast.78), kind=kOutput, calls=%fused_computation | convolution fusion | flops 226492704 | bytes 11534480 | tf_op jit(solution)/shard_map/et,eib->tib/dot_general | solution.py:35
  32.8 103.7 %all-reduce.2.cloned.1.call-done = f32[8,64,1024]{2,0,1:T(8,128)} async-done(((f32[8,64,1024]{2,0,1:T(8,128)}), f32[8,64,1024]{2,0,1:T(8,128)}) %all-reduce.2.cloned.1.call-update) | async-done | bytes 2097168 | tf_op jit(solution)/shard_map/psum | solution.py:38
  136.4 6.7 %fusion.9 = f32[8,64,64]{2,1,0:T(8,128)S(1)} fusion(f32[8,64,1024]{2,0,1:T(8,128)} %all-reduce.2.cloned.1.call-done), kind=kOutput, calls=%fused_computation.11 | convolution fusion | flops 402653184 | bytes 2228224 | tf_op jit(solution)/shard_map/tib,tjb->tij/dot_general | solution.py:39
  143.1 0.8 copy.26
  144.0 1.7 fusion.25
  145.7 47.6 %custom-call.8 = f32[8,64,64]{2,1,0:T(8,128)S(1)} custom-call(f32[8,64,64]{2,1,0:T(8,128)} %fusion.25), custom_call_target="Cholesky" | custom-call | tf_op jit(solution)/shard_map/jit(cholesky)/cholesky | solution.py:40
  193.4 0.8 select_bitcast_fusion
  194.3 40.3 %custom-call.9 = f32[8,1,64,64]{2,3,1,0:T(8,128)S(1)} custom-call(f32[8,1,64,64]{3,2,1,0:T(8,128)} %select_bitcast_fusion), custom_call_target="InvertDiagBlocksLowerTriangular" | custom-call | tf_op jit(solution)/shard_map/jit(_solve_triangular)/vmap()/triangular_solve | solution.py:41
  234.5 4.4 %fusion.42 = (bf16[8,64,1024]{2,1,0:T(8,128)(2,1)S(1)}, f32[8,64,1024]{2,1,0:T(8,128)}) fusion(f32[8,64,1024]{2,0,1:T(8,128)S(1)} %copy-done.1, f32[8,1,64,64]{2,3,1,0:T(8,128)S(1)} %custom-call.9), kind=kOutput, calls=%fused_computation.53 | convolution fusion | flops 403177472 | bytes 5373952 | tf_op jit(solution)/shard_map/jit(_solve_triangular)/vmap()/triangular_solve | solution.py:41
  238.9 1.6 convolution_convert_fusion.1
  240.5 5.5 %fusion.11 = f32[36,64,64]{1,2,0:T(8,128)S(1)} fusion(bf16[36,1,64,1024]{3,2,1,0:T(8,128)(2,1)} %param.7, bf16[36,64,1024]{2,0,1:T(8,128)(2,1)S(1)} %convolution_convert_fusion.1), kind=kOutput, calls=%fused_computation.14 | convolution fusion | flops 301989888 | bytes 10027008 | tf_op jit(solution)/shard_map/eib,ekb->eik/dot_general | solution.py:51
  246.0 0.5 copy.31
  246.5 0.8 fusion.16
  247.3 1.8 fusion.21
  249.1 2.3 convolution_bitcast_fusion
  251.5 1.7 dynamic-slice_multiply_fusion
  253.1 66.7 %reduce-scatter.2.cloned.1.call-done = f32[8,64,128]{2,1,0:T(8,128)} async-done(((f32[8,64,1024]{2,1,0:T(8,128)}), f32[8,64,128]{2,1,0:T(8,128)}) %reduce-scatter.2.cloned.1.call-update) | async-done | bytes 262160 | tf_op jit(solution)/shard_map/reduce_scatter | solution.py:58
  319.8 1.7 broadcast_multiply_fusion
  (27 shorter events, 1.3 us)
Async XLA Ops:
  7.2 8.2 %copy-start = (bf16[8,64,1024]{2,1,0:T(8,128)(2,1)S(1)}, bf16[8,64,1024]{2,1,0:T(8,128)(2,1)}, u32[]{:S(2)}) copy-start(bf16[8,64,1024]{2,1,0:T(8,128)(2,1)} %param.13) | copy-start | bytes 3145732
  7.2 8.9 %copy-start.4 = (f32[2,64,64]{2,1,0:T(8,128)S(1)}, f32[2,64,64]{2,1,0:T(8,128)}, u32[]{:S(2)}) copy-start(f32[2,64,64]{2,1,0:T(8,128)} %param.12) | copy-start | bytes 98308
  7.2 10.6 %copy-start.6 = (s32[36,1]{0,1:T(1,128)S(1)}, s32[36,1]{0,1:T(1,128)}, u32[]{:S(2)}) copy-start(s32[36,1]{0,1:T(1,128)} %param.8) | copy-start | bytes 436
  7.2 129.2 %all-reduce.2.cloned.1.call-start = ((), (), s32[]{:S(2)}) async-start(), calls=%async_computation.1 | async-start | bytes 4194304 | tf_op jit(solution)/shard_map/psum | solution.py:38
  15.4 0.7 copy-start.2
  18.8 3.8 %copy-start.5 = (s32[36,1]{0,1:T(1,128)S(1)}, s32[36,1]{0,1:T(1,128)}, u32[]{:S(2)}) copy-start(s32[36,1]{0,1:T(1,128)} %param.9) | copy-start | bytes 436
  32.7 287.2 %reduce-scatter.2.cloned.1.call-start = ((), (), s32[]{:S(2)}) async-start(), calls=%async_computation.2 | async-start | bytes 2359296 | tf_op jit(solution)/shard_map/reduce_scatter | solution.py:58
  136.4 98.1 %copy-start.1 = (f32[8,64,1024]{2,0,1:T(8,128)S(1)}, f32[8,64,1024]{2,0,1:T(8,128)}, u32[]{:S(2)}) copy-start(f32[8,64,1024]{2,0,1:T(8,128)} %all-reduce.2.cloned.1.call-done) | copy-start | bytes 6291460
  246.5 2.6 copy-start.3
Sparse Core Ops, SparseCore 0:
  32.8 103.5 all-reduce.1
  251.6 68.2 reduce-scatter.1
where the time goes:
time: 329 us; the launch traced here: 328 us
  waiting for transfers between devices  170 us (52%)
  other arithmetic  94.6 us (29%)
  matrix products  38.3 us (12%)
  between operations  14.9 us (5%)
  blocking collectives  7.42 us (2%)
    psum x1, waiting for transfers between devices, shards(): sketch_sum = lax.psum(sketch, 'wide')  104 us
    reduce_scatter x1, waiting for transfers between devices, shards(): lax.psum_scatter(partial_rows, 'wide', scatter_dimension=2, tiled=True)  66.7 us
    another operation x4, other arithmetic, shards(): lower_factor = jnp.linalg.cholesky(gram_matrix)  47.8 us
    another operation x3, other arithmetic, shards(): jax.scipy.linalg.solve_triangular(lower_factor, sketch_sum, lower=True)  41.1 us
    dot_general x1, matrix products, shards(): jnp.einsum('et,eib->tib', pick_target, contributions, precision=highest)  10.1 us
    all_gather x1, blocking collectives, shards(): gathered = lax.all_gather(panel_shared, 'narrow', axis=2, tiled=True)  7.42 us
    dot_general x1, matrix products, shards(): jnp.einsum('tib,tjb->tij', sketch_sum, sketch_sum, precision=highest)  6.7 us
  transfers between devices with their start and end apart: 2, of which 2 were waited for; matrix products, arithmetic and copies ran while one was open for 1% of the time, Pallas kernels for 0%

commit v1 on v0

--- a/solution.py
+++ b/solution.py
@@ -3,6 +3,18 @@
 import jax.numpy as jnp
 from jax import lax
 from jax.sharding import PartitionSpec as P
+
+
+def do_scales(vec):
+    amount_of = lax.axis_size("wide")
+    m_next, g_now = (vec, 0)
+    while 1 << g_now < amount_of:
+        mat_out = lax.ppermute(
+            m_next, axis_name="wide", perm=[(q, q ^ 1 << g_now) for q in range(amount_of)]
+        )
+        m_next = m_next + mat_out
+        g_now = g_now + 1
+    return m_next
 
 
 def shards(entry_factor, entry_panel, entry_target, entry_count, panel_shared, coupling, probes):
@@ -35,7 +47,7 @@
     sketch = jnp.einsum("et,eib->tib", pick_target, contributions, precision=highest)
     wide_count = lax.axis_size("wide")
     share_cols = full_width // wide_count
-    sketch_sum = lax.psum(sketch, "wide")
+    sketch_sum = do_scales(sketch)
     gram_matrix = jnp.einsum("tib,tjb->tij", sketch_sum, sketch_sum, precision=highest)
     lower_factor = jnp.linalg.cholesky(gram_matrix)
     basis = jax.scipy.linalg.solve_triangular(lower_factor, sketch_sum, lower=True)

time: 329 us -> 412 us (1.25)
  waiting for transfers between devices: 170 us -> 250 us
  starting transfers between devices: 0.08 us -> 6.01 us
    ppermute x0 -> x3, waiting for transfers between devices: none -> 181 us  [do_scales(): lax.ppermute(m_next, axis_name='wide', perm=[(q, q ^ 1 << g_now) for q in...]
    psum x1 -> x0, waiting for transfers between devices: 104 us -> none  [shards(): sketch_sum = lax.psum(sketch, 'wide')]
    ppermute x0 -> x3, starting transfers between devices: none -> 5.97 us  [do_scales(): lax.ppermute(m_next, axis_name='wide', perm=[(q, q ^ 1 << g_now) for q in...]
  transfers between devices with their start and end apart: 2 -> 4, of which waited for: 2 -> 4; matrix products, arithmetic and copies ran while one was open for 1% -> 0% of each run, Pallas kernels for 0% -> 0%
where the time goes in v1:
time: 412 us
  waiting for transfers between devices  250 us (61%)
  other arithmetic  96 us (23%)
  matrix products  34.7 us (8%)
  between operations  14.9 us (4%)
  blocking collectives  7.42 us (2%)
  starting transfers between devices  6.01 us (1%)
    ppermute x3, waiting for transfers between devices, do_scales(): lax.ppermute(m_next, axis_name='wide', perm=[(q, q ^ 1 << g_now) for q in...  181 us
    reduce_scatter x1, waiting for transfers between devices, shards(): lax.psum_scatter(partial_rows, 'wide', scatter_dimension=2, tiled=True)  68.9 us
    another operation x4, other arithmetic, shards(): lower_factor = jnp.linalg.cholesky(gram_matrix)  47.8 us
    another operation x3, other arithmetic, shards(): jax.scipy.linalg.solve_triangular(lower_factor, sketch_sum, lower=True)  41.1 us
    dot_general x1, matrix products, shards(): jnp.einsum('et,eib->tib', pick_target, contributions, precision=highest)  8.9 us
  transfers between devices with their start and end apart: 4, of which 4 were waited for; matrix products, arithmetic and copies ran while one was open for 0% of the time, Pallas kernels for 0%

profile of v1, /device:TPU:0, one launch (start us, length us, event | category | flops | bytes accessed | tf_op | source)
XLA Modules:
  0.0 411.7 jit_solution(8059848365727552496)
XLA Ops:
  8.0 7.4 %all_gather.3 = bf16[2,64,1024]{2,1,0:T(8,128)(2,1)S(1)} all-gather(bf16[2,64,256]{2,1,0:T(8,128)(2,1)} %param.11), channel_id=1, replica_groups=mesh['wide'=8,'narrow'=4] {'narrow'}, dimensions={2}, use_global_device_ids=true | all-gather | bytes 327680 | tf_op jit(solution)/shard_map/all_gather | solution.py:36
  18.8 3.8 fusion.4
  22.6 8.9 %fusion = f32[8,64,1024]{2,0,1:T(8,128)S(1)} fusion(f32[36,64,1024]{2,1,0:T(8,128)S(1)} %fusion.4, s32[36]{0:T(128)S(1)} %bitcast.78), kind=kOutput, calls=%fused_computation | convolution fusion | flops 226492704 | bytes 11534480 | tf_op jit(solution)/shard_map/et,eib->tib/dot_general | solution.py:47
  31.5 1.6 collective-permute-start
  33.1 46.3 %collective-permute-done = f32[8,64,1024]{2,0,1:T(8,128)S(1)} collective-permute-done((f32[8,64,1024]{2,0,1:T(8,128)S(1)}, f32[8,64,1024]{2,0,1:T(8,128)S(1)}, u32[]{:S(2)}, u32[]{:S(2)}) %collective-permute-start) | collective-permute-done | bytes 2097184 | tf_op jit(solution)/shard_map/ppermute | solution.py:12
  79.8 1.7 collective-permute-start.1
  81.5 45.4 %collective-permute-done.1 = f32[8,64,1024]{2,0,1:T(8,128)S(1)} collective-permute-done((f32[8,64,1024]{2,0,1:T(8,128)S(1)}, f32[8,64,1024]{2,0,1:T(8,128)S(1)}, u32[]{:S(2)}, u32[]{:S(2)}) %collective-permute-start.1) | collective-permute-done | bytes 2097184 | tf_op jit(solution)/shard_map/ppermute | solution.py:12
  127.5 2.7 collective-permute-start.2
  130.2 89.4 %collective-permute-done.2 = f32[8,64,1024]{2,0,1:T(8,128)S(1)} collective-permute-done((f32[8,64,1024]{2,0,1:T(8,128)S(1)}, f32[8,64,1024]{2,0,1:T(8,128)S(1)}, u32[]{:S(2)}, u32[]{:S(2)}) %collective-permute-start.2) | collective-permute-done | bytes 2097184 | tf_op jit(solution)/shard_map/ppermute | solution.py:12
  219.9 4.4 %fusion.9 = f32[8,64,64]{2,1,0:T(8,128)S(1)} fusion(f32[8,64,1024]{2,0,1:T(8,128)S(1)} %add.28), kind=kOutput, calls=%fused_computation.11 | convolution fusion | flops 402653184 | bytes 2228224 | tf_op jit(solution)/shard_map/tib,tjb->tij/dot_general | solution.py:51
  224.3 0.8 copy.26
  225.1 1.7 fusion.25
  226.8 47.6 %custom-call.8 = f32[8,64,64]{2,1,0:T(8,128)S(1)} custom-call(f32[8,64,64]{2,1,0:T(8,128)} %fusion.25), custom_call_target="Cholesky" | custom-call | tf_op jit(solution)/shard_map/jit(cholesky)/cholesky | solution.py:52
  274.6 0.8 select_bitcast_fusion
  275.4 40.3 %custom-call.9 = f32[8,1,64,64]{2,3,1,0:T(8,128)S(1)} custom-call(f32[8,1,64,64]{3,2,1,0:T(8,128)} %select_bitcast_fusion), custom_call_target="InvertDiagBlocksLowerTriangular" | custom-call | tf_op jit(solution)/shard_map/jit(_solve_triangular)/vmap()/triangular_solve | solution.py:53
  315.7 4.4 %fusion.42 = (bf16[8,64,1024]{2,1,0:T(8,128)(2,1)S(1)}, f32[8,64,1024]{2,1,0:T(8,128)}) fusion(f32[8,64,1024]{2,0,1:T(8,128)S(1)} %add.28, f32[8,1,64,64]{2,3,1,0:T(8,128)S(1)} %custom-call.9), kind=kOutput, calls=%fused_computation.53 | convolution fusion | flops 403177472 | bytes 5373952 | tf_op jit(solution)/shard_map/jit(_solve_triangular)/vmap()/triangular_solve | solution.py:53
  320.1 1.6 convolution_convert_fusion.1
  321.7 5.5 %fusion.11 = f32[36,64,64]{1,2,0:T(8,128)S(1)} fusion(bf16[36,1,64,1024]{3,2,1,0:T(8,128)(2,1)} %param.7, bf16[36,64,1024]{2,0,1:T(8,128)(2,1)S(1)} %convolution_convert_fusion.1), kind=kOutput, calls=%fused_computation.14 | convolution fusion | flops 301989888 | bytes 10027008 | tf_op jit(solution)/shard_map/eib,ekb->eik/dot_general | solution.py:63
  327.6 0.8 fusion.16
  328.4 1.8 fusion.21
  330.2 2.3 convolution_bitcast_fusion
  332.6 1.7 dynamic-slice_multiply_fusion
  334.3 68.9 %reduce-scatter.2.cloned.1.call-done = f32[8,64,128]{2,1,0:T(8,128)} async-done(((f32[8,64,1024]{2,1,0:T(8,128)}), f32[8,64,128]{2,1,0:T(8,128)}) %reduce-scatter.2.cloned.1.call-update) | async-done | bytes 262160 | tf_op jit(solution)/shard_map/reduce_scatter | solution.py:70
  403.1 1.7 broadcast_multiply_fusion
  (31 shorter events, 5.5 us)
Async XLA Ops:
  7.2 8.2 %copy-start = (bf16[8,64,1024]{2,1,0:T(8,128)(2,1)S(1)}, bf16[8,64,1024]{2,1,0:T(8,128)(2,1)}, u32[]{:S(2)}) copy-start(bf16[8,64,1024]{2,1,0:T(8,128)(2,1)} %param.13) | copy-start | bytes 3145732
  7.2 8.9 %copy-start.3 = (f32[2,64,64]{2,1,0:T(8,128)S(1)}, f32[2,64,64]{2,1,0:T(8,128)}, u32[]{:S(2)}) copy-start(f32[2,64,64]{2,1,0:T(8,128)} %param.12) | copy-start | bytes 98308
  7.2 10.6 %copy-start.5 = (s32[36,1]{0,1:T(1,128)S(1)}, s32[36,1]{0,1:T(1,128)}, u32[]{:S(2)}) copy-start(s32[36,1]{0,1:T(1,128)} %param.8) | copy-start | bytes 436
  7.2 395.9 %reduce-scatter.2.cloned.1.call-start = ((), (), s32[]{:S(2)}) async-start(), calls=%async_computation.1 | async-start | bytes 2359296 | tf_op jit(solution)/shard_map/reduce_scatter | solution.py:70
  15.4 0.7 copy-start.1
  18.8 3.8 copy-start.4
  31.5 47.9 %collective-permute-start = (f32[8,64,1024]{2,0,1:T(8,128)S(1)}, f32[8,64,1024]{2,0,1:T(8,128)S(1)}, u32[]{:S(2)}, u32[]{:S(2)}) collective-permute-start(f32[8,64,1024]{2,0,1:T(8,128)S(1)} %fusion), channel_id=1, source_target_pairs={{0,4},{4,0},{8,12},{12,8},{16,20},{20,16},{24,28},{28,24},{1,5},{5... | collective-permute-start | bytes 6291464 | tf_op jit(solution)/shard_map/ppermute | solution.py:12
  79.8 47.1 %collective-permute-start.1 = (f32[8,64,1024]{2,0,1:T(8,128)S(1)}, f32[8,64,1024]{2,0,1:T(8,128)S(1)}, u32[]{:S(2)}, u32[]{:S(2)}) collective-permute-start(f32[8,64,1024]{2,0,1:T(8,128)S(1)} %add.26), channel_id=1, source_target_pairs={{0,8},{4,12},{8,0},{12,4},{16,24},{20,28},{24,16},{28,20},{1,9},{5... | collective-permute-start | bytes 6291464 | tf_op jit(solution)/shard_map/ppermute | solution.py:12
  127.5 92.1 %collective-permute-start.2 = (f32[8,64,1024]{2,0,1:T(8,128)S(1)}, f32[8,64,1024]{2,0,1:T(8,128)S(1)}, u32[]{:S(2)}, u32[]{:S(2)}) collective-permute-start(f32[8,64,1024]{2,0,1:T(8,128)S(1)} %add.27), channel_id=1, source_target_pairs={{0,16},{4,20},{8,24},{12,28},{16,0},{20,4},{24,8},{28,12},{1,17},{... | collective-permute-start | bytes 6291464 | tf_op jit(solution)/shard_map/ppermute | solution.py:12
  327.6 2.6 copy-start.2
Sparse Core Ops, SparseCore 0:
  332.7 70.3 reduce-scatter.1
